TPU v7x, 128 devices: a whole 4x4x4 slice. The times are simulated.
128 devices in a mesh: row: 8 (over x_hi, y), col: 16 (over x_lo, z, core).
Axes of the slice: x: 4 (x_hi: 2, x_lo: 2; x = x_hi * 2 + x_lo), y: 4, z: 4, core: 2. Of those that a mesh axis runs over, the one named last changes fastest.
Arguments:
- matrix: float32 [32768, 8192], P('row', 'col'), may hold values from -6 to 6
- pivots: int32 [1024], replicated, may hold values from 0 to 32767, as said below
- lower_panel: float32 [1024, 32768], P('col', 'row'), as said below
Outputs:
- updated: float32 [32768, 8192], P('row', 'col')
Inputs may be any that keep to these rules, and one draw needn't show every extreme that they name: `pivots`: the 1024 entries are distinct rows of the trailing matrix. For column index r < 1024: lower_panel[r, r] = 1 and lower_panel[k, r] = 0 for k > r.
All inputs are finite; a program needn't handle non-finite values.
Results may differ from a plain program's by a relative error of at most 0.000059.
Values sent between devices are 32-bit elements; how exact they have to be, the bound alone decides.
No kernel may reach another device: no remote copies, remote signals or barrier semaphores. Data moves between devices by JAX's collectives and lax.ppermute only.
A program may use at most 128 MiB of HBM per device.

v0:
```python
import jax
import jax.numpy as jnp
from jax import lax
from jax.sharding import PartitionSpec as P


def spread(value, axis, source):
    kept = jnp.where(lax.axis_index(axis) == source, value, 0).astype(value.dtype)
    return lax.psum(kept, axis)


def displaced_rows(pivots, top):
    whole = jnp.arange(top, dtype=jnp.int32)
    chosen_top = jnp.any(pivots[None, :] == whole[:, None], axis=1)
    spare_rows = jnp.sort(jnp.where(chosen_top, jnp.int32(2**30), whole))
    vacated = jnp.sort(jnp.where(pivots >= top, pivots, jnp.int32(2**30)))
    return (spare_rows, vacated)


def contract(left_block, right_block):
    return lax.dot_general(
        left_block,
        right_block,
        (((0,), (0,)), ((), ())),
        precision=lax.Precision.HIGHEST,
        preferred_element_type=jnp.float32,
    )


def per_device(matrix, pivots, lower_panel):
    top = pivots.shape[0]
    local_rows, local_cols = matrix.shape
    first_row = lax.axis_index("row") * local_rows
    spare_rows, vacated = displaced_rows(pivots, top)
    initial_top = spread(matrix[:top], "row", 0)
    inside = (vacated >= first_row) & (vacated < first_row + local_rows)
    local_target = jnp.where(inside, vacated - first_row, local_rows)
    swapped = matrix.at[local_target].set(
        initial_top[jnp.minimum(spare_rows, top - 1)], mode="drop"
    )
    owned_mask = (pivots >= first_row) & (pivots < first_row + local_rows)
    local_index = jnp.clip(pivots - first_row, 0, local_rows - 1)
    picked = jnp.where(owned_mask[:, None], jnp.take(matrix, local_index, axis=0), 0.0)
    pivot_block = lax.psum(picked, "row")
    product = contract(lax.all_gather(lower_panel, "col", axis=0, tiled=True), pivot_block)
    global_rows = first_row + jnp.arange(local_rows, dtype=jnp.int32)[:, None]
    return jnp.where(global_rows < top, product, swapped - product)


def solution(mesh):
    in_specs = (P("row", "col"), P(), P("col", "row"))
    out_specs = P("row", "col")
    return jax.shard_map(
        per_device, mesh=mesh, in_specs=in_specs, out_specs=out_specs, check_vma=False
    )
```

profile of v0, /device:TPU:1, one launch (start us, length us, event | category | flops | bytes accessed | tf_op | source)
XLA Modules:
  0.0 292.9 jit_solution(3470179886124595553)
XLA Ops:
  7.4 0.0 all-reduce.3.cloned.1.call-start
  7.4 0.0 copy-start.1
  7.4 7.8 %copy.12 = f32[4096,512]{1,0:T(8,128)} copy(f32[4096,512]{1,0:T(8,128)} %param.3) | data formatting | bytes 16777216
  15.1 0.0 copy-done.1
  15.2 7.4 %gather_fusion = f32[1024,512]{1,0:T(8,128)S(1)} fusion(f32[4096,512]{1,0:T(8,128)} %copy.12, s32[1024]{0:T(1024)S(1)} %get-tuple-element.15), kind=kCustom, calls=%fused_computation | custom fusion | bytes 4198400 | tf_op jit(solution)/shard_map/jit(_take)/gather | solution.py:43
  22.6 3.1 %slice_select_fusion = f32[1024,512]{1,0:T(8,128)} fusion(f32[4096,512]{1,0:T(8,128)} %copy.12, pred[]{:T(512)S(6)} %eq.16), kind=kLoop, calls=%fused_computation.8 | loop fusion | flops 524288 | bytes 4194305 | tf_op jit(solution)/shard_map/jit(_where)/select_n | solution.py:8
  25.7 2.0 select_select_fusion
  27.7 0.0 all-reduce.3.cloned.1.call-update
  27.7 0.0 all-gather.2.cloned.1.call-start
  27.7 0.5 all-gather.2.cloned.1.call-update
  28.3 4.4 %sort.21 = (s32[1024]{0:T(1024)S(1)}, s32[1024]{0:T(1024)}) sort(s32[1024]{0:T(1024)S(1)} %get-tuple-element.16, s32[1024]{0:T(1024)S(1)} %iota.18), dimensions={0}, to_apply=%region_1.2 | sort | flops 10240 | bytes 16384 | tf_op jit(solution)/shard_map/jit(sort)/sort | solution.py:16
  32.6 0.6 fusion
  33.2 4.4 %sort.28 = (s32[1024]{0:T(1024)S(1)}, s32[1024]{0:T(1024)}) sort(s32[1024]{0:T(1024)S(1)} %iota_select_fusion, s32[1024]{0:T(1024)S(1)} %iota.20), dimensions={0}, to_apply=%region_4.5 | sort | flops 10240 | bytes 16384 | tf_op jit(solution)/shard_map/jit(sort)/sort | solution.py:15
  37.6 178.3 %all-reduce.3.cloned.1.call-done = (f32[1024,512]{1,0:T(8,128)}, f32[1024,512]{1,0:T(8,128)}) async-done(((f32[1024,512]{1,0:T(8,128)}, f32[1024,512]{1,0:T(8,128)}), (f32[1024,512]{1,0:T(8,128)}, f32[1024,512]{1,0:T(8,128)})) %all-reduce.3.cloned.1.call-update) | async-done | bytes 4194320 | tf_op jit(solution)/shard_map/psum | solution.py:9
  215.9 20.3 %scatter_custom_fusion = f32[4096,512]{1,0:T(8,128)} fusion(f32[4096,512]{1,0:T(8,128)} %copy.12, s32[1024]{0:T(1024)S(1)} %get-tuple-element.17, f32[1024,512]{1,0:T(8,128)} %get-tuple-element.11, s32[1024]{0:T(1024)S(1)} %get-tuple-element.18), kind=kCustom, calls=%fused_computation.6 | custom fusion | bytes 8388608 | tf_op jit(solution)/shard_map/scatter | solution.py:38
  236.1 0.0 copy-start
  236.1 9.1 %copy.6 = f32[4096,512]{0,1:T(8,128)} copy(f32[4096,512]{1,0:T(8,128)} %scatter_custom_fusion) | data formatting | bytes 16777216 | tf_op jit(solution)/shard_map/scatter | solution.py:38
  245.2 0.0 all-gather.2.cloned.1.call-done
  245.2 0.0 copy-done
  245.2 31.4 %subtract_select_fusion = f32[4096,512]{0,1:T(8,128)} fusion(f32[4096,512]{0,1:T(8,128)} %copy.6, f32[1024,512]{1,0:T(8,128)S(1)} %copy-done, f32[1024,4096]{1,0:T(8,128)} %all-gather.2.cloned.1.call-done, pred[4096]{0:T(1024)(128)(4,1)S(1)} %add_compare_fusion), kind=kOutput, calls=%fused_computation.3 | convolution fusion | flops 25773998080 | bytes 35655680 | tf_op jit(solution)/shard_map/dot_general | solution.py:21
  276.6 8.9 %copy.7 = f32[4096,512]{1,0:T(8,128)} copy(f32[4096,512]{0,1:T(8,128)} %subtract_select_fusion) | data formatting | bytes 16777216 | tf_op jit(solution)/shard_map/jit(_where)/select_n | solution.py:47
  (7 shorter events, 0.1 us)
Async XLA Ops:
  7.4 208.5 %all-reduce.3.cloned.1.call-start = ((), (), s32[]{:S(2)}) async-start(), calls=%async_computation.1 | async-start | bytes 8388608 | tf_op jit(solution)/shard_map/psum | solution.py:9
  7.4 7.8 %copy-start.1 = (s32[1024]{0:T(1024)S(1)}, s32[1024]{0:T(1024)}, u32[]{:S(2)}) copy-start(s32[1024]{0:T(1024)} %param.4) | copy-start | bytes 12292
  27.7 217.5 %all-gather.2.cloned.1.call-start = ((), (), s32[]{:S(2)}) async-start(), calls=%async_computation | async-start | bytes 17825792 | tf_op jit(solution)/shard_map/all_gather | solution.py:45
  236.1 9.1 %copy-start = (f32[1024,512]{1,0:T(8,128)S(1)}, f32[1024,512]{1,0:T(8,128)}, u32[]{:S(2)}) copy-start(f32[1024,512]{1,0:T(8,128)} %get-tuple-element.12) | copy-start | bytes 6291460
Sparse Core Ops, SparseCore 0:
  27.8 187.9 all-reduce.2
Sparse Core Ops, SparseCore 1:
  29.9 131.6 all-gather.1
where the time goes:
time: 294 us; the launch traced here: 293 us
  waiting for transfers between devices  179 us (61%)
  local copies, waits for them, and re-layouts  53.4 us (18%)
  matrix products  31.4 us (11%)
  between operations  14.9 us (5%)
  other arithmetic  14.4 us (5%)
    psum x1, waiting for transfers between devices, spread(): return lax.psum(kept, axis)  178 us
    dot_general x1, matrix products, contract(): lax.dot_general(left_block, right_block, (((0,), (0,)), ((), ())), precis...  31.4 us
    scatter x2, local copies, waits for them, and re-layouts, per_device(): matrix.at[local_target]  29.3 us
    select_n x1, local copies, waits for them, and re-layouts, per_device(): return jnp.where(global_rows < top, product, swapped - product)  8.94 us
    unnamed x5, local copies, waits for them, and re-layouts  7.78 us
    gather x1, local copies, waits for them, and re-layouts, per_device(): jnp.take(matrix, local_index, axis=0)  7.4 us
  transfers between devices with their start and end apart: 2, of which 1 were waited for; matrix products, arithmetic and copies ran while one was open for 13% of the time, Pallas kernels for 0%

commit v1 on v0

--- a/solution.py
+++ b/solution.py
@@ -6,7 +6,7 @@
 
 def spread(value, axis, source):
     kept = jnp.where(lax.axis_index(axis) == source, value, 0).astype(value.dtype)
-    return lax.psum(kept, axis)
+    return jnp.sum(lax.all_gather(kept, axis), axis=0)
 
 
 def displaced_rows(pivots, top):

time: 294 us -> 437 us (1.49)
  waiting for transfers between devices: 179 us -> 319 us
  other arithmetic: 14.4 us -> 22.5 us
  local copies, waits for them, and re-layouts: 53.4 us -> 48.9 us
    all_gather x0 -> x1, waiting for transfers between devices: none -> 165 us  [spread(): return jnp.sum(lax.all_gather(kept, axis), axis=0)]
    psum x1, waiting for transfers between devices: 178 us -> 56.9 us  [per_device(): pivot_block = lax.psum(picked, 'row')]
    all_gather x1, waiting for transfers between devices: 0.01 us -> 97.2 us  [per_device(): lax.all_gather(lower_panel, 'col', axis=0, tiled=True)]
    reduce_sum x0 -> x1, other arithmetic: none -> 8.08 us  [spread(): return jnp.sum(lax.all_gather(kept, axis), axis=0)]
    scatter x2, local copies, waits for them, and re-layouts: 29.3 us -> 24.2 us  [per_device(): matrix.at[local_target]]
  transfers between devices with their start and end apart: 2 -> 3, of which waited for: 1 -> 3; matrix products, arithmetic and copies ran while one was open for 13% -> 12% of each run, Pallas kernels for 0% -> 0%
where the time goes in v1:
time: 437 us; the launch traced here: 436 us
  waiting for transfers between devices  319 us (73%)
  local copies, waits for them, and re-layouts  48.9 us (11%)
  matrix products  31.9 us (7%)
  other arithmetic  22.5 us (5%)
  between operations  13.2 us (3%)
    all_gather x1, waiting for transfers between devices, spread(): return jnp.sum(lax.all_gather(kept, axis), axis=0)  165 us
    all_gather x1, waiting for transfers between devices, per_device(): lax.all_gather(lower_panel, 'col', axis=0, tiled=True)  97.2 us
    psum x1, waiting for transfers between devices, per_device(): pivot_block = lax.psum(picked, 'row')  56.9 us
    dot_general x1, matrix products, contract(): lax.dot_general(left_block, right_block, (((0,), (0,)), ((), ())), precis...  31.9 us
    scatter x2, local copies, waits for them, and re-layouts, per_device(): matrix.at[local_target]  24.2 us
    select_n x1, local copies, waits for them, and re-layouts, per_device(): return jnp.where(global_rows < top, product, swapped - product)  8.94 us
  transfers between devices with their start and end apart: 3, of which 3 were waited for; matrix products, arithmetic and copies ran while one was open for 12% of the time, Pallas kernels for 0%

profile of v1, /device:TPU:1, one launch (start us, length us, event | category | flops | bytes accessed | tf_op | source)
XLA Modules:
  0.0 436.1 jit_solution(6153441311114188784)
XLA Ops:
  6.5 0.0 all-gather.6.cloned.1.call-start
  6.5 7.8 %copy.11 = f32[4096,512]{1,0:T(8,128)} copy(f32[4096,512]{1,0:T(8,128)} %param.3) | data formatting | bytes 16777216
  14.3 3.1 slice_select_fusion
  17.4 0.0 copy-start
  17.4 0.0 all-gather.6.cloned.1.call-update
  17.4 0.0 all-reduce.2.cloned.1.call-start
  17.5 0.6 copy-done
  18.1 7.4 %gather_fusion = f32[1024,512]{1,0:T(8,128)S(1)} fusion(f32[4096,512]{1,0:T(8,128)} %copy.11, s32[1024]{0:T(1024)S(1)} %get-tuple-element.13), kind=kCustom, calls=%fused_computation | custom fusion | bytes 4198400 | tf_op jit(solution)/shard_map/jit(_take)/gather | solution.py:43
  25.5 2.0 select_select_fusion
  27.5 0.0 all-reduce.2.cloned.1.call-update
  27.5 0.0 all-gather.4.cloned.1.call-start
  27.6 0.7 all-gather.4.cloned.1.call-update
  28.3 4.4 %sort.21 = (s32[1024]{0:T(1024)S(1)}, s32[1024]{0:T(1024)}) sort(s32[1024]{0:T(1024)S(1)} %get-tuple-element.14, s32[1024]{0:T(1024)S(1)} %iota.18), dimensions={0}, to_apply=%region_1.2 | sort | flops 10240 | bytes 16384 | tf_op jit(solution)/shard_map/jit(sort)/sort | solution.py:16
  32.7 0.6 fusion
  33.2 4.4 %sort.28 = (s32[1024]{0:T(1024)S(1)}, s32[1024]{0:T(1024)}) sort(s32[1024]{0:T(1024)S(1)} %iota_select_fusion, s32[1024]{0:T(1024)S(1)} %iota.20), dimensions={0}, to_apply=%region_4.5 | sort | flops 10240 | bytes 16384 | tf_op jit(solution)/shard_map/jit(sort)/sort | solution.py:15
  37.6 164.5 %all-gather.6.cloned.1.call-done = f32[8192,512]{1,0:T(8,128)} async-done(((f32[1024,512]{1,0:T(8,128)}), f32[8192,512]{1,0:T(8,128)}) %all-gather.6.cloned.1.call-update) | async-done | bytes 16777232 | tf_op jit(solution)/shard_map/all_gather | solution.py:9
  202.2 8.1 %reduce_sum.9 = f32[1024,512]{1,0:T(8,128)S(1)} reduce(f32[8,1024,512]{2,1,0:T(8,128)} %bitcast.5, f32[]{:T(128)} %constant.18.clone.1), dimensions={0}, to_apply=%region_2.3 | reduce | flops 3670016 | bytes 18874372 | tf_op jit(solution)/shard_map/reduce_sum | solution.py:9
  210.2 15.3 %scatter_custom_fusion = f32[4096,512]{1,0:T(8,128)} fusion(f32[4096,512]{1,0:T(8,128)} %copy.11, s32[1024]{0:T(1024)S(1)} %compare_select_fusion.1, f32[1024,512]{1,0:T(8,128)S(1)} %reduce_sum.9, s32[1024]{0:T(1024)S(1)} %fusion.3), kind=kCustom, calls=%fused_computation.6 | custom fusion | bytes 8388608 | tf_op jit(solution)/shard_map/scatter | solution.py:38
  225.5 8.9 %copy.6 = f32[4096,512]{0,1:T(8,128)} copy(f32[4096,512]{1,0:T(8,128)} %scatter_custom_fusion) | data formatting | bytes 16777216 | tf_op jit(solution)/shard_map/scatter | solution.py:38
  234.5 56.9 %all-reduce.2.cloned.1.call-done = f32[1024,512]{1,0:T(8,128)} async-done(((f32[1024,512]{1,0:T(8,128)}), f32[1024,512]{1,0:T(8,128)}) %all-reduce.2.cloned.1.call-update) | async-done | bytes 2097168 | tf_op jit(solution)/shard_map/psum | solution.py:44
  291.4 97.2 %all-gather.4.cloned.1.call-done = f32[1024,4096]{1,0:T(8,128)} async-done(((f32[64,4096]{1,0:T(8,128)}), f32[1024,4096]{1,0:T(8,128)}) %all-gather.4.cloned.1.call-update) | async-done | bytes 16777232 | tf_op jit(solution)/shard_map/all_gather | solution.py:45
  388.7 31.9 %subtract_select_fusion = f32[4096,512]{0,1:T(8,128)} fusion(f32[4096,512]{0,1:T(8,128)} %copy.6, f32[1024,512]{1,0:T(8,128)} %all-reduce.2.cloned.1.call-done, f32[1024,4096]{1,0:T(8,128)} %all-gather.4.cloned.1.call-done, pred[4096]{0:T(1024)(128)(4,1)S(1)} %add_compare_fusion), kind=kOutput, calls=%fused_computation.3 | convolution fusion | flops 25773998080 | bytes 35655680 | tf_op jit(solution)/shard_map/dot_general | solution.py:21
  420.6 8.9 %copy.7 = f32[4096,512]{1,0:T(8,128)} copy(f32[4096,512]{0,1:T(8,128)} %subtract_select_fusion) | data formatting | bytes 16777216 | tf_op jit(solution)/shard_map/jit(_where)/select_n | solution.py:47
  (8 shorter events, 0.1 us)
Async XLA Ops:
  6.5 195.6 %all-gather.6.cloned.1.call-start = ((), (), s32[]{:S(2)}) async-start(), calls=%async_computation.2 | async-start | bytes 18874368 | tf_op jit(solution)/shard_map/all_gather | solution.py:9
  17.4 0.7 copy-start
  17.4 274.0 %all-reduce.2.cloned.1.call-start = ((), (), s32[]{:S(2)}) async-start(), calls=%async_computation | async-start | bytes 4194304 | tf_op jit(solution)/shard_map/psum | solution.py:44
  27.5 361.1 %all-gather.4.cloned.1.call-start = ((), (), s32[]{:S(2)}) async-start(), calls=%async_computation.1 | async-start | bytes 17825792 | tf_op jit(solution)/shard_map/all_gather | solution.py:45
Sparse Core Ops, SparseCore 0:
  17.6 184.5 all-gather.5
  204.7 86.7 all-reduce.1
  293.1 95.4 all-gather.3
